TPU v7x, 32 devices: a whole 2x2x4 slice. The times are simulated.
32 devices in a mesh: grp: 2 (over x), chan: 4 (over y, core), ctx: 4 (over z).
Axes of the slice: x: 2, y: 2, z: 4, core: 2. Of those that a mesh axis runs over, the one named last changes fastest.
Arguments:
- features: bfloat16 [4096, 4096], P(('grp', 'ctx'), 'chan'), parts along dimension 0, may hold values from -6 to 6
- filter_taps: bfloat16 [2048, 4096], P(None, 'chan'), may hold values from -0.125 to 0.125
- skip_gain: float32 [4096], P('chan'), may hold values from -4 to 4
- in_weight: bfloat16 [4096, 3, 4096], P(None, None, 'chan'), may hold values from -0.09375 to 0.09375
- out_weight: bfloat16 [4096, 4096], P(None, 'chan'), may hold values from -0.125 to 0.125
Outputs:
- layer_out: bfloat16 [4096, 4096], P(('grp', 'ctx'), 'chan'), parts along dimension 0
There are 2 independent parts, one for each index of `grp`. A program takes and returns all parts, laid end to end along the dimension named above; an argument that names none is the same for every part. Nothing has to cross between parts.
All inputs are finite; a program needn't handle non-finite values.
Results may differ from a plain program's by a relative error of at most 0.013.
Values may be sent and summed in bfloat16 or wider, within the bound.
No kernel may reach another device: no remote copies, remote signals or barrier semaphores. Data moves between devices by JAX's collectives and lax.ppermute only.
A program may use at most 320 MiB of HBM per device.

v0:
```python
import math
import jax
import jax.numpy as jnp
from jax import lax
from jax.sharding import PartitionSpec as P

P_SIZE = 128


def dft_tables(block_len):
    period = 2 * block_len
    freq_col = jnp.arange(period, dtype=jnp.int32)[:, None]
    place_row = jnp.arange(period, dtype=jnp.int32)[None, :]
    angles = (freq_col * place_row % period).astype(jnp.float32) * (2.0 * math.pi / period)
    forward = jnp.concatenate([jnp.cos(angles), -jnp.sin(angles)], axis=0).astype(jnp.bfloat16)
    out_place = jnp.arange(block_len, dtype=jnp.int32)[:, None] + block_len
    angle_out = (out_place * place_row % period).astype(jnp.float32) * (2.0 * math.pi / period)
    inverse = (jnp.concatenate([jnp.cos(angle_out), -jnp.sin(angle_out)], axis=1) / period).astype(
        jnp.bfloat16
    )
    return (forward, inverse)


def input_spectra(token_rows, forward):
    channels = token_rows.shape[1]
    grouped = token_rows.reshape(token_rows.shape[0] // P_SIZE, P_SIZE, channels)
    spectra = jnp.einsum(
        "fp,bpc->bfc", forward[:, :P_SIZE], grouped, preferred_element_type=jnp.float32
    )
    return spectra.astype(jnp.bfloat16)


def segment_spectra(padded, forward):
    channels = padded.shape[1]
    count = padded.shape[0] // P_SIZE - 1
    tap_blocks = padded.reshape(count + 1, P_SIZE, channels)
    segments = jnp.concatenate([tap_blocks[:-1], tap_blocks[1:]], axis=1)
    spectra = jnp.einsum("fn,knc->kfc", forward, segments, preferred_element_type=jnp.float32)
    return spectra.astype(jnp.bfloat16)


def shards(features, filter_taps, skip_gain, in_weight, out_weight):
    forward, inverse = dft_tables(P_SIZE)
    channels = in_weight.shape[2]
    tok_rows = features.shape[0]
    per_dev = tok_rows // P_SIZE
    period = 2 * P_SIZE
    total_blocks = per_dev * lax.axis_size("ctx")
    first_mine = lax.axis_index("ctx") * per_dev
    last_mine = first_mine + per_dev - 1
    padded_all = jnp.concatenate([jnp.zeros((P_SIZE, channels), jnp.bfloat16), filter_taps], axis=0)
    lag_spectra = segment_spectra(padded_all, forward)
    flipped = jnp.concatenate([lag_spectra[::-1], jnp.zeros_like(lag_spectra)], axis=0)
    flat_in = in_weight.reshape(in_weight.shape[0], 3 * channels)
    weight_slice = flat_in
    projected = jnp.dot(
        lax.all_gather(features, "chan", axis=1, tiled=True),
        weight_slice,
        preferred_element_type=jnp.float32,
    )
    query_rows = projected[:, :channels].astype(jnp.bfloat16)
    mixed_in = (projected[:, channels : 2 * channels] * projected[:, 2 * channels :]).astype(
        jnp.bfloat16
    )

    def add_spectra(running, source):
        source_re = source[:, :period].astype(jnp.float32)
        source_im = source[:, period:].astype(jnp.float32)
        outputs = []
        for out_block in range(per_dev):
            start_lag = total_blocks - 1 - (first_mine + out_block)
            window = lax.dynamic_slice_in_dim(flipped, start_lag, source.shape[0], 0).astype(
                jnp.float32
            )
            lag_re = window[:, :period]
            lag_im = window[:, period:]
            out_re = jnp.sum(lag_re * source_re - lag_im * source_im, axis=0)
            out_im = jnp.sum(lag_re * source_im + lag_im * source_re, axis=0)
            outputs.append(jnp.concatenate([out_re, out_im], axis=0))
        return running + jnp.stack(outputs)

    zero_spectra = jnp.zeros((per_dev, 2 * period, channels), jnp.float32)
    portion = lax.all_gather(mixed_in, "ctx", axis=0, tiled=True)
    first_in = jnp.int32(0) // P_SIZE

    def accumulate(current):
        return add_spectra(current, input_spectra(portion, forward))

    summed = lax.cond(first_in <= last_mine, accumulate, lambda current: current, zero_spectra)
    block_spectra = summed.astype(jnp.bfloat16)
    conv_out = jnp.einsum(
        "tf,bfc->btc", inverse, block_spectra, preferred_element_type=jnp.float32
    ).reshape(tok_rows, channels)
    gated_rows = (
        query_rows.astype(jnp.float32)
        * (conv_out + skip_gain[None, :] * mixed_in.astype(jnp.float32))
    ).astype(jnp.bfloat16)
    weight_slice = out_weight
    layer_out = jnp.dot(
        lax.all_gather(gated_rows, "chan", axis=1, tiled=True),
        weight_slice,
        preferred_element_type=jnp.float32,
    )
    return layer_out.astype(jnp.bfloat16)


def solution(mesh):
    return jax.shard_map(
        shards,
        mesh=mesh,
        in_specs=(
            P(("grp", "ctx"), "chan"),
            P(None, "chan"),
            P("chan"),
            P(None, None, "chan"),
            P(None, "chan"),
        ),
        out_specs=P(("grp", "ctx"), "chan"),
        check_vma=False,
    )
```

profile of v0, /device:TPU:0, one launch (start us, length us, event | category | flops | bytes accessed | tf_op | source)
XLA Modules:
  0.0 333.9 jit_solution(129528146827862470)
XLA Ops:
  6.5 0.0 all-gather.4.cloned.1.call-start
  6.5 0.7 all-gather.4.cloned.1.call-update
  7.3 0.0 all-gather.6.cloned.1.call-start
  7.3 31.7 %copy.13 = bf16[4096,3,1024]{0,2,1:T(8,128)(2,1)} copy(bf16[4096,3,1024]{2,0,1:T(8,128)(2,1)} %param.10) | data formatting | bytes 50331648 | tf_op args[3]
  39.0 7.1 %all-gather.4.cloned.1.call-done = bf16[512,4096]{1,0:T(8,128)(2,1)} async-done(((bf16[512,1024]{1,0:T(8,128)(2,1)}), bf16[512,4096]{1,0:T(8,128)(2,1)}) %all-gather.4.cloned.1.call-update) | async-done | bytes 4194320 | tf_op jit(solution)/shard_map/all_gather | solution.py:57
  46.1 17.9 %fusion.50 = f32[512,3072]{1,0:T(8,128)S(1)} fusion(bf16[512,4096]{1,0:T(8,128)(2,1)} %all-gather.4.cloned.1.call-done, bf16[4096,3072]{0,1:T(8,128)(2,1)} %bitcast.39), kind=kOutput, calls=%fused_computation.93 | convolution fusion | flops 12884901888 | bytes 35651584 | tf_op jit(solution)/shard_map/dot_general | solution.py:56
  64.0 0.0 copy-start
  64.0 2.6 copy-done
  66.6 1.3 fusion.25
  67.9 0.0 all-gather.6.cloned.1.call-update
  67.9 0.0 all-gather.8.cloned.1.call-start
  67.9 4.5 %pad_slice_fusion = bf16[2048,1024]{1,0:T(8,128)(2,1)} fusion(bf16[2048,1024]{1,0:T(8,128)(2,1)} %param.8), kind=kLoop, calls=%fused_computation.52 | loop fusion | bytes 8388608 | tf_op jit(solution)/shard_map/slice | solution.py:37
  72.4 6.5 %copy.14 = bf16[16,128,1024]{1,2,0:T(8,128)(2,1)} copy(bf16[16,128,1024]{2,1,0:T(8,128)(2,1)} %bitcast.41) | data formatting | bytes 8388608 | tf_op jit(solution)/shard_map/slice | solution.py:37
  78.9 6.4 %copy.15 = bf16[16,128,1024]{1,2,0:T(8,128)(2,1)} copy(bf16[16,128,1024]{2,1,0:T(8,128)(2,1)} %bitcast.40) | data formatting | bytes 8388608 | tf_op jit(solution)/shard_map/slice | solution.py:37
  85.3 1.1 negate_convert_fusion
  86.4 10.4 %convert_bitcast_fusion.1 = bf16[16,512,1024]{1,2,0:T(8,128)(2,1)} fusion(bf16[16,128,1024]{1,2,0:T(8,128)(2,1)} %copy.15, bf16[16,128,1024]{1,2,0:T(8,128)(2,1)} %copy.14, bf16[256,256]{1,0:T(8,128)(2,1)S(1)} %get-tuple-element.49, bf16[256,256]{1,0:T(8,128)(2,1)S(1)} %get-tuple-element.50), kind=kOutput, calls=%fused_computation.48 | convolution fusion | flops 4320657408 | bytes 25427968 | tf_op jit(solution)/shard_map/fn,knc->kfc/dot_general | solution.py:38
  96.8 13.8 %rev.3 = bf16[16,512,1024]{1,2,0:T(8,128)(2,1)} reverse(bf16[16,512,1024]{1,2,0:T(8,128)(2,1)} %convert_bitcast_fusion.1), dimensions={0} | reverse | bytes 33554432 | tf_op jit(solution)/shard_map/rev | solution.py:53
  110.6 1.2 fusion.46
  111.8 36.9 %all-gather.6.cloned.1.call-done = bf16[2048,1024]{1,0:T(8,128)(2,1)} async-done(((bf16[512,1024]{1,0:T(8,128)(2,1)}), bf16[2048,1024]{1,0:T(8,128)(2,1)}) %all-gather.6.cloned.1.call-update) | async-done | bytes 4194320 | tf_op jit(solution)/shard_map/all_gather | solution.py:83
  148.8 110.0 %conditional.1 = (bf16[4,512,1024]{1,2,0:T(8,128)(2,1)}) conditional(s32[]{:T(128)} %convert_element_type.68, () %tuple.13, (bf16[16,512,1024]{1,2,0:T(8,128)(2,1)}, s32[]{:T(128)}, bf16[2048,1024]{1,0:T(8,128)(2,1)}, bf16[512,256]{1,0:T(8,128)(2,1)S(1)}) %tuple.14), branch_computations={%region_0.1_spmd, %region_1.10_spmd} | conditional | flops 2344615936 | bytes 344064256 | solution.py:89
  148.8 45.6 %fusion.18 = (f32[16,512,1024]{1,2,0:T(8,128)}, f32[16,512,1024]{1,2,0:T(8,128)}, f32[16,512,1024]{1,2,0:T(8,128)}, f32[16,512,1024]{1,2,0:T(8,128)}) fusion(s32[]{:T(128)S(6)} %select_n.25, bf16[16,512,1024]{1,2,0:T(8,128)(2,1)} %get-tuple-element.19, s32[]{:T(128)S(6)} %select_n.24, s32[]{:T(128)S(6)} %select_n.26, s32[]{:T(128)S(6)} %select_n.23), kind=kLoop, calls=%fused_computation.38 | loop fusion | flops 33554432 | bytes 150994960 | tf_op jit(solution)/shard_map/cond/branch_1_fun/convert_element_type | solution.py:72
  194.3 10.4 %convert_bitcast_fusion = bf16[16,512,1024]{1,2,0:T(8,128)(2,1)} fusion(bf16[16,128,1024]{2,1,0:T(8,128)(2,1)} %bitcast.42, bf16[512,256]{1,0:T(8,128)(2,1)S(1)} %get-tuple-element.22), kind=kOutput, calls=%fused_computation.40 | convolution fusion | flops 2155872256 | bytes 21102592 | tf_op jit(solution)/shard_map/cond/branch_1_fun/fp,bpc->bfc/dot_general | solution.py:27
  204.8 49.9 %fusion.5 = (bf16[256,1024]{0,1:T(8,128)(2,1)S(1)}, bf16[256,1024]{0,1:T(8,128)(2,1)S(1)}, bf16[256,1024]{0,1:T(8,128)(2,1)S(1)}, bf16[256,1024]{0,1:T(8,128)(2,...) fusion(f32[16,512,1024]{1,2,0:T(8,128)} %get-tuple-element.40, ...), kind=kLoop, calls=%fused_computation.25 | loop fusion | flops 140509184 | bytes 155189248 | tf_op jit(solution)/shard_map/cond/branch_1_fun/reduce_sum | solution.py:77
  254.7 1.4 maximum_bitcast_fusion
  256.1 0.2 maximum_bitcast_fusion.2
  256.3 2.5 pad_maximum_fusion
  258.7 0.0 copy-start.1
  258.7 3.7 %fusion.40 = f32[4,1024,128]{1,2,0:T(8,128)S(1)} fusion(bf16[4,512,1024]{1,2,0:T(8,128)(2,1)} %get-tuple-element.51, f32[128,256]{1,0:T(8,128)} %get-tuple-element.48, f32[128,256]{1,0:T(8,128)S(1)} %get-tuple-element.47), kind=kOutput, calls=%fused_computation.82 | convolution fusion | flops 537067520 | bytes 6553600 | tf_op jit(solution)/shard_map/tf,bfc->btc/dot_general | solution.py:91
  262.4 0.0 copy-done.1
  262.4 4.7 %fusion.27 = bf16[512,1024]{1,0:T(8,128)(2,1)} fusion(f32[4,1024,128]{1,2,0:T(8,128)S(1)} %fusion.40, f32[512,3072]{1,0:T(8,128)} %copy-done, f32[1024]{0:T(1024)S(1)} %copy-done.1), kind=kLoop, calls=%fused_computation.58 | loop fusion | flops 4194304 | bytes 8392704 | tf_op jit(solution)/shard_map/convert_element_type | solution.py:97
  267.1 0.0 all-gather.8.cloned.1.call-update
  267.1 50.1 %all-gather.8.cloned.1.call-done = bf16[512,4096]{1,0:T(8,128)(2,1)} async-done(((bf16[512,1024]{1,0:T(8,128)(2,1)}), bf16[512,4096]{1,0:T(8,128)(2,1)}) %all-gather.8.cloned.1.call-update) | async-done | bytes 4194320 | tf_op jit(solution)/shard_map/all_gather | solution.py:100
  317.2 10.1 %convolution_convert_fusion = bf16[512,1024]{1,0:T(8,128)(2,1)} fusion(bf16[512,4096]{1,0:T(8,128)(2,1)} %all-gather.8.cloned.1.call-done, bf16[4096,1024]{1,0:T(8,128)(2,1)} %param.11), kind=kOutput, calls=%fused_computation.59 | convolution fusion | flops 4295491584 | bytes 13631488 | tf_op jit(solution)/shard_map/dot_general | solution.py:99
  (2 shorter events, 0.0 us)
Async XLA Ops:
  6.5 39.6 %all-gather.4.cloned.1.call-start = ((), (), s32[]{:S(2)}) async-start(), calls=%async_computation | async-start | bytes 5242880 | tf_op jit(solution)/shard_map/all_gather | solution.py:57
  7.3 141.5 %all-gather.6.cloned.1.call-start = ((), (), s32[]{:S(2)}) async-start(), calls=%async_computation.1 | async-start | bytes 5242880 | tf_op jit(solution)/shard_map/all_gather | solution.py:83
  64.0 2.6 copy-start
  67.9 249.4 %all-gather.8.cloned.1.call-start = ((), (), s32[]{:S(2)}) async-start(), calls=%async_computation.2 | async-start | bytes 5242880 | tf_op jit(solution)/shard_map/all_gather | solution.py:100
  258.7 3.7 %copy-start.1 = (f32[1024]{0:T(1024)S(1)}, f32[1024]{0:T(1024)}, u32[]{:S(2)}) copy-start(f32[1024]{0:T(1024)} %param.9) | copy-start | bytes 12292
Sparse Core Ops, SparseCore 0:
  8.9 37.1 all-gather.3
  68.0 80.7 all-gather.5
  267.3 49.9 all-gather.7
where the time goes:
time: 335 us; the launch traced here: 334 us
  other arithmetic  108 us (32%)
  waiting for transfers between devices  94.9 us (28%)
  local copies, waits for them, and re-layouts  65.4 us (20%)
  matrix products  52.5 us (16%)
  between operations  13.2 us (4%)
    all_gather x1, waiting for transfers between devices, shards(): lax.all_gather(gated_rows, 'chan', axis=1, tiled=True)  50.1 us
    reduce_sum x1, other arithmetic, add_spectra(): out_re = jnp.sum(lag_re * source_re - lag_im * source_im, axis=0)  49.9 us
    convert_element_type x1, other arithmetic, add_spectra(): lax.dynamic_slice_in_dim(flipped, start_lag, source.shape[0], 0)  45.6 us
    all_gather x1, waiting for transfers between devices, shards(): portion = lax.all_gather(mixed_in, 'ctx', axis=0, tiled=True)  36.9 us
    unnamed x5, local copies, waits for them, and re-layouts  34.3 us
    dot_general x1, matrix products, shards(): jnp.dot(lax.all_gather(features, 'chan', axis=1, tiled=True), weight_slic...  17.9 us
    slice x3, local copies, waits for them, and re-layouts, segment_spectra(): segments = jnp.concatenate([tap_blocks[:-1], tap_blocks[1:]], axis=1)  17.3 us
    rev x1, local copies, waits for them, and re-layouts, shards(): lag_spectra[::-1]  13.8 us
  transfers between devices with their start and end apart: 3, of which 3 were waited for; matrix products, arithmetic and copies ran while one was open for 23% of the time, Pallas kernels for 0%

commit v1 on v0

--- a/solution.py
+++ b/solution.py
@@ -5,6 +5,16 @@
 from jax.sharding import PartitionSpec as P
 
 P_SIZE = 128
+
+
+def turned_line(x, name, dim):
+    size = lax.axis_size(name)
+    held, tiles = (x, [x])
+    for _ in range(size - 1):
+        held = lax.ppermute(held, name, [(i, (i + 1) % size) for i in range(size)])
+        tiles.insert(0, held)
+    flat = jnp.concatenate(tiles, axis=dim)
+    return jnp.roll(flat, (lax.axis_index(name) + 1) * x.shape[dim], axis=dim)
 
 
 def dft_tables(block_len):
@@ -80,7 +90,7 @@
         return running + jnp.stack(outputs)
 
     zero_spectra = jnp.zeros((per_dev, 2 * period, channels), jnp.float32)
-    portion = lax.all_gather(mixed_in, "ctx", axis=0, tiled=True)
+    portion = turned_line(mixed_in, "ctx", 0)
     first_in = jnp.int32(0) // P_SIZE
 
     def accumulate(current):

time: 335 us -> 354 us (1.057)
  local copies, waits for them, and re-layouts: 65.4 us -> 77.4 us
  other arithmetic: 108 us -> 112 us
    all_gather x1 -> x0, waiting for transfers between devices: 36.9 us -> none  [shards(): portion = lax.all_gather(mixed_in, 'ctx', axis=0, tiled=True)]
    ppermute x0 -> x3, waiting for transfers between devices: none -> 35.8 us  [turned_line(): held = lax.ppermute(held, name, [(i, (i + 1) % size) for i in range(size)])]
    unnamed x5 -> x17, local copies, waits for them, and re-layouts: 34.3 us -> 43.1 us
    dynamic_slice x0 -> x1, local copies, waits for them, and re-layouts: none -> 5.4 us  [turned_line(): return jnp.roll(flat, (lax.axis_index(name) + 1) * x.shape[dim], axis=dim)]
    unnamed x0 -> x2, other arithmetic: none -> 3.71 us
  transfers between devices with their start and end apart: 3 -> 5, of which waited for: 3 -> 5; matrix products, arithmetic and copies ran while one was open for 23% -> 21% of each run, Pallas kernels for 0% -> 0%
where the time goes in v1:
time: 354 us; the launch traced here: 353 us
  other arithmetic  112 us (32%)
  waiting for transfers between devices  95.7 us (27%)
  local copies, waits for them, and re-layouts  77.4 us (22%)
  matrix products  52.5 us (15%)
  between operations  13.5 us (4%)
    all_gather x1, waiting for transfers between devices, shards(): lax.all_gather(gated_rows, 'chan', axis=1, tiled=True)  52.1 us
    reduce_sum x1, other arithmetic, add_spectra(): out_re = jnp.sum(lag_re * source_re - lag_im * source_im, axis=0)  50.2 us
    convert_element_type x1, other arithmetic, add_spectra(): lax.dynamic_slice_in_dim(flipped, start_lag, source.shape[0], 0)  45.5 us
    unnamed x17, local copies, waits for them, and re-layouts  43.1 us
    ppermute x3, waiting for transfers between devices, turned_line(): held = lax.ppermute(held, name, [(i, (i + 1) % size) for i in range(size)])  35.8 us
    dot_general x1, matrix products, shards(): jnp.dot(lax.all_gather(features, 'chan', axis=1, tiled=True), weight_slic...  18 us
    slice x3, local copies, waits for them, and re-layouts, segment_spectra(): segments = jnp.concatenate([tap_blocks[:-1], tap_blocks[1:]], axis=1)  15.2 us
    rev x1, local copies, waits for them, and re-layouts, shards(): lag_spectra[::-1]  13.7 us
  transfers between devices with their start and end apart: 5, of which 5 were waited for; matrix products, arithmetic and copies ran while one was open for 21% of the time, Pallas kernels for 0%

profile of v1, /device:TPU:0, one launch (start us, length us, event | category | flops | bytes accessed | tf_op | source)
XLA Modules:
  0.0 352.6 jit_solution(5538351282623654144)
XLA Ops:
  6.5 0.0 all-gather.3.cloned.1.call-start
  6.5 0.7 all-gather.3.cloned.1.call-update
  7.3 0.0 all-gather.5.cloned.1.call-start
  7.3 31.6 %copy.12 = bf16[4096,3,1024]{0,2,1:T(8,128)(2,1)} copy(bf16[4096,3,1024]{2,0,1:T(8,128)(2,1)} %param.10) | data formatting | bytes 50331648 | tf_op args[3]
  38.9 7.2 %all-gather.3.cloned.1.call-done = bf16[512,4096]{1,0:T(8,128)(2,1)} async-done(((bf16[512,1024]{1,0:T(8,128)(2,1)}), bf16[512,4096]{1,0:T(8,128)(2,1)}) %all-gather.3.cloned.1.call-update) | async-done | bytes 4194320 | tf_op jit(solution)/shard_map/all_gather | solution.py:67
  46.1 0.0 copy-start.1
  46.1 18.0 %fusion.50 = f32[512,3072]{1,0:T(8,128)S(1)} fusion(bf16[512,4096]{1,0:T(8,128)(2,1)} %all-gather.3.cloned.1.call-done, bf16[4096,3072]{0,1:T(8,128)(2,1)} %bitcast.41), kind=kOutput, calls=%fused_computation.102 | convolution fusion | flops 12884901888 | bytes 35651584 | tf_op jit(solution)/shard_map/dot_general | solution.py:66
  64.1 0.0 copy-start
  64.1 2.7 copy-done
  66.8 0.3 fusion.25
  67.2 1.5 collective-permute-start
  68.7 25.6 %collective-permute-done = bf16[512,1024]{1,0:T(8,128)(2,1)S(1)} collective-permute-done((bf16[512,1024]{1,0:T(8,128)(2,1)S(1)}, bf16[512,1024]{1,0:T(8,128)(2,1)S(1)}, u32[]{:S(2)}, u32[]{:S(2)}) %collective-permute-start) | collective-permute-done | bytes 1048608 | tf_op jit(solution)/shard_map/ppermute | solution.py:14
  94.3 0.0 collective-permute-start.1
  94.3 0.0 copy-done.1
  94.3 2.4 pad_slice_fusion
  96.7 6.4 %copy.13 = bf16[16,128,1024]{1,2,0:T(8,128)(2,1)} copy(bf16[16,128,1024]{2,1,0:T(8,128)(2,1)} %bitcast.44) | data formatting | bytes 8388608 | tf_op jit(solution)/shard_map/slice | solution.py:47
  103.1 6.4 %copy.14 = bf16[16,128,1024]{1,2,0:T(8,128)(2,1)} copy(bf16[16,128,1024]{2,1,0:T(8,128)(2,1)} %bitcast.43) | data formatting | bytes 8388608 | tf_op jit(solution)/shard_map/slice | solution.py:47
  109.5 1.1 negate_convert_fusion
  110.6 10.0 %collective-permute-done.1 = bf16[512,1024]{1,0:T(8,128)(2,1)S(1)} collective-permute-done((bf16[512,1024]{1,0:T(8,128)(2,1)S(1)}, bf16[512,1024]{1,0:T(8,128)(2,1)S(1)}, u32[]{:S(2)}, u32[]{:S(2)}) %collective-permute-start.1) | collective-permute-done | bytes 1048608 | tf_op jit(solution)/shard_map/ppermute | solution.py:14
  120.6 0.0 collective-permute-start.2
  120.6 10.3 %convert_bitcast_fusion.1 = bf16[16,512,1024]{1,2,0:T(8,128)(2,1)} fusion(bf16[16,128,1024]{1,2,0:T(8,128)(2,1)} %copy.14, bf16[16,128,1024]{1,2,0:T(8,128)(2,1)} %copy.13, bf16[256,256]{1,0:T(8,128)(2,1)S(1)} %get-tuple-element.166, bf16[256,256]{1,0:T(8,128)(2,1)S(1)} %get-tuple-element.167), kind=kOutput, calls=%fused_computation.49 | convolution fusion | flops 4320657408 | bytes 25427968 | tf_op jit(solution)/shard_map/fn,knc->kfc/dot_general | solution.py:48
  130.9 13.7 %rev.3 = bf16[16,512,1024]{1,2,0:T(8,128)(2,1)} reverse(bf16[16,512,1024]{1,2,0:T(8,128)(2,1)} %convert_bitcast_fusion.1), dimensions={0} | reverse | bytes 33554432 | tf_op jit(solution)/shard_map/rev | solution.py:63
  144.6 1.2 fusion.46
  145.9 0.2 collective-permute-done.2
  146.0 2.3 constant_dynamic-update-slice_fusion.7
  148.3 1.1 constant_dynamic-update-slice_fusion.6
  149.4 1.1 constant_dynamic-update-slice_fusion.5
  150.4 3.7 %constant_dynamic-update-slice_fusion.4 = bf16[4096,1024]{1,0:T(8,128)(2,1)} fusion(bf16[4096,1024]{1,0:T(8,128)(2,1)} %constant_dynamic-update-slice_fusion.5, f32[512,3072]{1,0:T(8,128)} %copy-done), kind=kLoop, calls=%fused_computation.94 | loop fusion | flops 1048576 | bytes 5242880
  154.1 2.3 constant_dynamic-update-slice_fusion.3
  156.4 1.0 constant_dynamic-update-slice_fusion.2
  157.4 1.1 constant_dynamic-update-slice_fusion.1
  158.5 0.0 slice-done
  158.5 0.0 slice-done.1
  158.5 1.3 constant_dynamic-update-slice_fusion
  159.8 115.3 %conditional.1 = (bf16[4,512,1024]{1,2,0:T(8,128)(2,1)}) conditional(s32[]{:T(128)} %convert_element_type.92, () %tuple.24, (bf16[16,512,1024]{1,2,0:T(8,128)(2,1)}, s32[]{:T(128)}, s32[]{:T(128)}, s32[]{:T(128)}, bf16[4096,1024]{1,0:T(8,128)(2,1)}, /*index=5*/bf16[512,256]{1,0:T(8,128)(2,1)S(1)}, s32[]{:T(128)}, s32[]{:T(128)}) %tuple.28), branch_computations={%region_0.1_spmd, %region_1.10_spmd.clone} | conditional | flops 2344615936 | bytes 352453056 | solution.py:99
  159.8 5.4 %constant_dynamic-slice_fusion = bf16[2048,1024]{1,0:T(8,128)(2,1)} fusion(bf16[4096,1024]{1,0:T(8,128)(2,1)} %get-tuple-element.124, s32[]{:T(128)S(6)} %select_n.66), kind=kLoop, calls=%fused_computation.48 | loop fusion | bytes 8388612 | tf_op jit(solution)/shard_map/jit(_roll_dynamic)/dynamic_slice | solution.py:17
  165.2 10.4 %convert_bitcast_fusion = bf16[16,512,1024]{1,2,0:T(8,128)(2,1)} fusion(bf16[16,128,1024]{2,1,0:T(8,128)(2,1)} %bitcast.42, bf16[512,256]{1,0:T(8,128)(2,1)S(1)} %get-tuple-element.126), kind=kOutput, calls=%fused_computation.40 | convolution fusion | flops 2155872256 | bytes 21102592 | tf_op jit(solution)/shard_map/cond/branch_1_fun/fp,bpc->bfc/dot_general | solution.py:37
  175.7 45.5 %fusion.18 = (f32[16,512,1024]{1,2,0:T(8,128)}, f32[16,512,1024]{1,2,0:T(8,128)}, f32[16,512,1024]{1,2,0:T(8,128)}, f32[16,512,1024]{1,2,0:T(8,128)}) fusion(s32[]{:T(128)S(6)} %select_n.68, bf16[16,512,1024]{1,2,0:T(8,128)(2,1)} %get-tuple-element.122, s32[]{:T(128)S(6)} %select_n.67, s32[]{:T(128)S(6)} %select_n.69, s32[]{:T(128)S(6)} %select_n.64), kind=kLoop, calls=%fused_computation.38 | loop fusion | flops 33554432 | bytes 150994960 | tf_op jit(solution)/shard_map/cond/branch_1_fun/convert_element_type | solution.py:82
  221.2 50.2 %fusion.5 = (bf16[256,1024]{0,1:T(8,128)(2,1)S(1)}, bf16[256,1024]{0,1:T(8,128)(2,1)S(1)}, bf16[256,1024]{0,1:T(8,128)(2,1)S(1)}, bf16[256,1024]{0,1:T(8,128)(2,...) fusion(f32[16,512,1024]{1,2,0:T(8,128)} %get-tuple-element.157,, ...), kind=kLoop, calls=%fused_computation.25 | loop fusion | flops 140509184 | bytes 155189248 | tf_op jit(solution)/shard_map/cond/branch_1_fun/reduce_sum | solution.py:87
  271.4 1.4 maximum_bitcast_fusion
  272.7 0.2 maximum_bitcast_fusion.2
  272.9 2.2 pad_maximum_fusion
  275.1 3.7 %fusion.40 = f32[4,1024,128]{1,2,0:T(8,128)S(1)} fusion(bf16[4,512,1024]{1,2,0:T(8,128)(2,1)} %get-tuple-element.168, f32[128,256]{1,0:T(8,128)} %get-tuple-element.165, f32[128,256]{1,0:T(8,128)S(1)} %get-tuple-element.164), kind=kOutput, calls=%fused_computation.83 | convolution fusion | flops 537067520 | bytes 6553600 | tf_op jit(solution)/shard_map/tf,bfc->btc/dot_general | solution.py:101
  278.8 0.0 copy-done.2
  278.8 4.7 %fusion.27 = bf16[512,1024]{1,0:T(8,128)(2,1)} fusion(f32[4,1024,128]{1,2,0:T(8,128)S(1)} %fusion.40, f32[512,3072]{1,0:T(8,128)} %copy-done, f32[1024]{0:T(1024)S(1)} %copy-done.2), kind=kLoop, calls=%fused_computation.59 | loop fusion | flops 4194304 | bytes 8392704 | tf_op jit(solution)/shard_map/convert_element_type | solution.py:107
  283.5 0.0 all-gather.5.cloned.1.call-update
  283.5 52.1 %all-gather.5.cloned.1.call-done = bf16[512,4096]{1,0:T(8,128)(2,1)} async-done(((bf16[512,1024]{1,0:T(8,128)(2,1)}), bf16[512,4096]{1,0:T(8,128)(2,1)}) %all-gather.5.cloned.1.call-update) | async-done | bytes 4194320 | tf_op jit(solution)/shard_map/all_gather | solution.py:110
  335.6 10.1 %convolution_convert_fusion = bf16[512,1024]{1,0:T(8,128)(2,1)} fusion(bf16[512,4096]{1,0:T(8,128)(2,1)} %all-gather.5.cloned.1.call-done, bf16[4096,1024]{1,0:T(8,128)(2,1)} %param.11), kind=kOutput, calls=%fused_computation.60 | convolution fusion | flops 4295491584 | bytes 13631488 | tf_op jit(solution)/shard_map/dot_general | solution.py:109
  (6 shorter events, 0.0 us)
Async XLA Ops:
  6.5 39.6 %all-gather.3.cloned.1.call-start = ((), (), s32[]{:S(2)}) async-start(), calls=%async_computation | async-start | bytes 5242880 | tf_op jit(solution)/shard_map/all_gather | solution.py:67
  7.3 328.4 %all-gather.5.cloned.1.call-start = ((), (), s32[]{:S(2)}) async-start(), calls=%async_computation.1 | async-start | bytes 5242880 | tf_op jit(solution)/shard_map/all_gather | solution.py:110
  46.1 48.2 %copy-start.1 = (bf16[2048,1024]{1,0:T(8,128)(2,1)S(1)}, bf16[2048,1024]{1,0:T(8,128)(2,1)}, u32[]{:S(2)}) copy-start(bf16[2048,1024]{1,0:T(8,128)(2,1)} %param.8) | copy-start | bytes 12582916
  64.1 2.7 copy-start
  67.2 27.2 %collective-permute-start = (bf16[512,1024]{1,0:T(8,128)(2,1)S(1)}, bf16[512,1024]{1,0:T(8,128)(2,1)S(1)}, u32[]{:S(2)}, u32[]{:S(2)}) collective-permute-start(bf16[512,1024]{1,0:T(8,128)(2,1)S(1)} %fusion.25), channel_id=1, source_target_pairs={{0,1},{1,2},{2,3},{3,0},{4,5},{5,6},{6,7},{7,4},{8,9},{9,10},{10,1... | collective-permute-start | bytes 3145736 | tf_op jit(solution)/shard_map/ppermute | solution.py:14
  94.3 26.2 %collective-permute-start.1 = (bf16[512,1024]{1,0:T(8,128)(2,1)S(1)}, bf16[512,1024]{1,0:T(8,128)(2,1)S(1)}, u32[]{:S(2)}, u32[]{:S(2)}) collective-permute-start(bf16[512,1024]{1,0:T(8,128)(2,1)S(1)} %collective-permute-done), channel_id=1, source_target_pairs={{0,1},{1,2},{2,3},{3,0},{4,5},{5,6},{6,7},{7,4},{8,9},{9,10},{10,1... | collective-permute-start | bytes 3145736 | tf_op jit(solution)/shard_map/ppermute | solution.py:14
  120.6 25.5 %collective-permute-start.2 = (bf16[512,1024]{1,0:T(8,128)(2,1)S(1)}, bf16[512,1024]{1,0:T(8,128)(2,1)}, u32[]{:S(2)}, u32[]{:S(2)}) collective-permute-start(bf16[512,1024]{1,0:T(8,128)(2,1)S(1)} %collective-permute-done.1), channel_id=1, source_target_pairs={{0,1},{1,2},{2,3},{3,0},{4,5},{5,6},{6,7},{7,4},{8,9},{9,10},{10,1... | collective-permute-start | bytes 3145736 | tf_op jit(solution)/shard_map/ppermute | solution.py:14
  148.3 10.2 %slice-start = ((s8[6291456]{0:T(1024)(128)(4,1)}), s8[4194304]{0:T(1024)(128)(4,1)S(1)}, s32[]{:S(2)}) async-start(s8[6291456]{0:T(1024)(128)(4,1)} %bitcast.39), calls=%async_computation.2 | async-start | bytes 8388608
  150.4 8.1 %slice-start.1 = ((s8[6291456]{0:T(1024)(128)(4,1)}), s8[2097152]{0:T(1024)(128)(4,1)S(1)}, s32[]{:S(2)}) async-start(s8[6291456]{0:T(1024)(128)(4,1)} %bitcast.39), calls=%async_computation.3 | async-start | bytes 4194304
  275.1 3.7 %copy-start.2 = (f32[1024]{0:T(1024)S(1)}, f32[1024]{0:T(1024)}, u32[]{:S(2)}) copy-start(f32[1024]{0:T(1024)} %param.9) | copy-start | bytes 12292
Sparse Core Ops, SparseCore 0:
  8.9 37.1 all-gather.2
  283.7 51.9 all-gather.4
